TPU v7x, 512 devices: a whole 4x8x8 slice. The times are simulated.
512 devices in a mesh: grp: 4 (over y_lo, core), src: 16 (over y_hi, x), rcv: 8 (over z).
Axes of the slice: x: 4, y: 8 (y_hi: 4, y_lo: 2; y = y_hi * 2 + y_lo), z: 8, core: 2. Of those that a mesh axis runs over, the one named last changes fastest.
Arguments:
- recorded: bfloat16 [4, 2, 4096, 4096], P('grp', None, 'src', 'rcv'), parts along dimension 0, as said below
- aperture: int32 [128, 32, 3], P(('grp', 'src'), 'rcv'), parts along dimension 0, may hold values from 0 to 32, as said below
Outputs:
- multiples: float32 [4, 2, 4096, 4096], P('grp', None, 'src', 'rcv'), parts along dimension 0
There are 4 independent parts, one for each index of `grp`. A program takes and returns all parts, laid end to end along the dimension named above; each array names one. Nothing has to cross between parts.
Inputs may be any that keep to these rules, and one draw needn't show every extreme that they name: The data obey reciprocity: recorded(f, c, q, j) equals recorded(f, c, j, q). `aperture`: field 1 is from 4 to 32, field 0 plus field 1 is at most 32, field 2 is from 0 to 2. In every draw some tile pair spans all 32 k-blocks and some has taper width 2.
All inputs are finite; a program needn't handle non-finite values.
Results may differ from a plain program's by a relative error of at most 0.0004.
Values may be sent and summed in bfloat16 or wider, within the bound.
No kernel may reach another device: no remote copies, remote signals or barrier semaphores. Data moves between devices by JAX's collectives and lax.ppermute only.
A program may use at most 64 MiB of HBM per device.

v0:
```python
import jax
import jax.numpy as jnp
from jax import lax
from jax.sharding import PartitionSpec as P

NB = 32
TILE = 128


def tile_weights(aperture):
    block_ids = jnp.arange(NB, dtype=jnp.int32)
    offset = block_ids[None, None, :] - aperture[..., 0:1]
    extent = aperture[..., 1:2]
    taper_width = aperture[..., 2:3]
    margin = jnp.minimum(offset, extent - 1 - offset)
    ramped = jnp.minimum(
        1.0, (margin + 1).astype(jnp.float32) / (taper_width + 1).astype(jnp.float32)
    )
    return jnp.where((offset >= 0) & (offset < extent), ramped, 0.0)


def shards(recorded, aperture):
    slices = recorded.shape[0]
    own_rows = recorded.shape[2]
    own_cols = recorded.shape[3]
    row_tiles = own_rows // TILE
    col_tiles = own_cols // TILE
    weights = tile_weights(aperture)
    block_ids = jnp.arange(NB, dtype=jnp.int32)
    left_panel = lax.all_gather(recorded, "rcv", axis=3, tiled=True)

    def block_terms(incoming, first_row, span_rows, tile_weight):
        part_left = lax.dynamic_slice_in_dim(left_panel, first_row, span_rows, 3)
        part_left = part_left.reshape(slices, 2, row_tiles, TILE, span_rows)
        block_of = (first_row + jnp.arange(span_rows, dtype=jnp.int32)) // TILE
        row_weights = jnp.sum(
            jnp.where(block_of[:, None] == block_ids[None, :], tile_weight[:, :, None, :], 0.0),
            axis=-1,
        )
        scaled = (part_left[:, :, :, None, :, :] * row_weights[None, None, :, :, None, :]).astype(
            jnp.bfloat16
        )
        sub_tiles = tile_weight.shape[1]
        right_tiles = incoming.reshape(slices, 2, span_rows, sub_tiles, TILE)
        products = jnp.einsum(
            "fastik,fbktj->fabstij", scaled, right_tiles, preferred_element_type=jnp.float32
        )
        return jnp.stack(
            [products[:, 0, 0] - products[:, 1, 1], products[:, 0, 1] + products[:, 1, 0]], 1
        )

    empty = jnp.zeros((slices, 2, row_tiles, col_tiles, TILE, TILE), jnp.float32)
    incoming = lax.all_gather(recorded, "src", axis=2, tiled=True)
    extent = incoming.shape[2]

    def add_block(first_row, span_rows, running):
        portion = lax.dynamic_slice_in_dim(incoming, first_row, span_rows, 2)
        return running + block_terms(portion, first_row, span_rows, weights)

    sweeps = extent // TILE
    summed = lax.fori_loop(
        0, sweeps, lambda number, running: add_block(number * TILE, TILE, running), empty
    )
    return summed.transpose(0, 1, 2, 4, 3, 5).reshape(slices, 2, own_rows, own_cols)


def solution(mesh):
    in_specs = (P("grp", None, "src", "rcv"), P(("grp", "src"), "rcv", None))
    out_specs = P("grp", None, "src", "rcv")
    return jax.shard_map(shards, mesh=mesh, in_specs=in_specs, out_specs=out_specs, check_vma=False)
```

profile of v0, /device:TPU:1, one launch (start us, length us, event | category | flops | bytes accessed | tf_op | source)
XLA Modules:
  0.0 312.6 jit_solution(3568070417147690657)
XLA Ops:
  7.3 2.0 copy.15
  10.1 63.1 %all-gather.5.cloned.1.call-done = bf16[1,2,256,4096]{3,2,1,0:T(8,128)(2,1)} async-done(((bf16[1,2,256,512]{3,2,1,0:T(8,128)(2,1)}), bf16[1,2,256,4096]{3,2,1,0:T(8,128)(2,1)}) %all-gather.5.cloned.1.call-update) | async-done | bytes 4194320 | tf_op jit(solution)/shard_map/all_gather | solution.py:30
  73.2 131.2 %all-gather.3.cloned.1.call-done = bf16[1,2,4096,512]{2,3,1,0:T(8,128)(2,1)} async-done(((bf16[1,2,256,512]{2,3,1,0:T(8,128)(2,1)}), bf16[1,2,4096,512]{2,3,1,0:T(8,128)(2,1)}) %all-gather.3.cloned.1.call-update) | async-done | bytes 8388624 | tf_op jit(solution)/shard_map/all_gather | solution.py:53
  204.4 99.5 %while.16 = (s32[]{:T(128)}, f32[1,2,2,4,128,128]{4,5,2,3,1,0:T(8,128)S(1)}, bf16[1,2,4096,512]{2,3,1,0:T(8,128)(2,1)}, bf16[1,2,256,4096]{3,2,1,0:T(8,128)(2,1)...) while((s32[]{:T(128)}, ...), condition=%wide.region_2.3_spmd.clone, body=%wide.region_0.2_spmd.clone.sunk | while | flops 135929600 | bytes 10120505 | solution.py:61
  205.4 1.0 constant_dynamic-slice_fusion.5
  208.5 1.0 constant_dynamic-slice_fusion.5
  211.6 1.0 constant_dynamic-slice_fusion.5
  214.7 1.0 constant_dynamic-slice_fusion.5
  217.8 1.0 constant_dynamic-slice_fusion.5
  220.9 1.0 constant_dynamic-slice_fusion.5
  224.0 1.0 constant_dynamic-slice_fusion.5
  227.1 1.0 constant_dynamic-slice_fusion.5
  230.2 1.0 constant_dynamic-slice_fusion.5
  233.4 1.0 constant_dynamic-slice_fusion.5
  236.5 1.0 constant_dynamic-slice_fusion.5
  239.6 1.0 constant_dynamic-slice_fusion.5
  242.7 1.0 constant_dynamic-slice_fusion.5
  245.8 1.0 constant_dynamic-slice_fusion.5
  248.9 1.0 constant_dynamic-slice_fusion.5
  252.0 1.0 constant_dynamic-slice_fusion.5
  255.1 1.0 constant_dynamic-slice_fusion.5
  258.3 1.0 constant_dynamic-slice_fusion.5
  267.6 1.0 constant_dynamic-slice_fusion.5
  273.8 1.0 constant_dynamic-slice_fusion.5
  276.9 1.0 constant_dynamic-slice_fusion.5
  280.0 1.0 constant_dynamic-slice_fusion.5
  283.1 1.0 constant_dynamic-slice_fusion.5
  286.3 1.0 constant_dynamic-slice_fusion.5
  289.4 1.0 constant_dynamic-slice_fusion.5
  295.6 1.0 constant_dynamic-slice_fusion.5
  301.8 1.0 constant_dynamic-slice_fusion.5
  304.4 1.4 reshape.136
  (364 shorter events, 72.1 us)
Async XLA Ops:
  6.5 66.7 %all-gather.5.cloned.1.call-start = ((), (), s32[]{:S(2)}) async-start(), calls=%async_computation.1 | async-start | bytes 4718592 | tf_op jit(solution)/shard_map/all_gather | solution.py:30
  7.3 197.1 %all-gather.3.cloned.1.call-start = ((), (), s32[]{:S(2)}) async-start(), calls=%async_computation | async-start | bytes 8912896 | tf_op jit(solution)/shard_map/all_gather | solution.py:53
Sparse Core Ops, SparseCore 0:
  9.4 63.7 all-gather.4
  76.2 128.1 all-gather.2
where the time goes:
time: 314 us; the launch traced here: 313 us
  waiting for transfers between devices  195 us (62%)
  local copies, waits for them, and re-layouts  64.6 us (21%)
  other arithmetic  22.6 us (7%)
  matrix products  13.9 us (4%)
  between operations  13.4 us (4%)
    all_gather x1, waiting for transfers between devices, shards(): incoming = lax.all_gather(recorded, 'src', axis=2, tiled=True)  131 us
    all_gather x1, waiting for transfers between devices, shards(): left_panel = lax.all_gather(recorded, 'rcv', axis=3, tiled=True)  63.1 us
    dynamic_slice x32, local copies, waits for them, and re-layouts, add_block(): portion = lax.dynamic_slice_in_dim(incoming, first_row, span_rows, 2)  31.2 us
    dynamic_slice x32, local copies, waits for them, and re-layouts, block_terms(): part_left = lax.dynamic_slice_in_dim(left_panel, first_row, span_rows, 3)  29.4 us
    dot_general x32, matrix products, block_terms(): jnp.einsum('fastik,fbktj->fabstij', scaled, right_tiles, preferred_elemen...  13.9 us
    add x32, other arithmetic, add_block(): return running + block_terms(portion, first_row, span_rows, weights)  10.7 us
  transfers between devices with their start and end apart: 2, of which 2 were waited for; matrix products, arithmetic and copies ran while one was open for 1% of the time, Pallas kernels for 0%

commit v1 on v0

--- a/solution.py
+++ b/solution.py
@@ -27,7 +27,8 @@
     col_tiles = own_cols // TILE
     weights = tile_weights(aperture)
     block_ids = jnp.arange(NB, dtype=jnp.int32)
-    left_panel = lax.all_gather(recorded, "rcv", axis=3, tiled=True)
+    copies = jnp.concatenate([recorded] * lax.axis_size("rcv"), axis=3)
+    left_panel = lax.all_to_all(copies, "rcv", 3, 3, tiled=True)
 
     def block_terms(incoming, first_row, span_rows, tile_weight):
         part_left = lax.dynamic_slice_in_dim(left_panel, first_row, span_rows, 3)

time: 314 us -> 263 us (0.84)
  waiting for transfers between devices: 195 us -> 116 us
  local copies, waits for them, and re-layouts: 64.6 us -> 82.3 us
  starting transfers between devices: 0.04 us -> 11 us
    all_gather x1, waiting for transfers between devices: 131 us -> 18.9 us  [shards(): incoming = lax.all_gather(recorded, 'src', axis=2, tiled=True)]
    all_to_all x0 -> x1, waiting for transfers between devices: none -> 96.8 us  [shards(): left_panel = lax.all_to_all(copies, 'rcv', 3, 3, tiled=True)]
    all_gather x1 -> x0, waiting for transfers between devices: 63.1 us -> none  [shards(): left_panel = lax.all_gather(recorded, 'rcv', axis=3, tiled=True)]
    all_to_all x0 -> x1, starting transfers between devices: none -> 11 us  [shards(): left_panel = lax.all_to_all(copies, 'rcv', 3, 3, tiled=True)]
    unnamed x1 -> x11, local copies, waits for them, and re-layouts: 2.04 us -> 11.5 us
    dynamic_slice x32 -> x64, local copies, waits for them, and re-layouts: 29.4 us -> 36.4 us  [block_terms(): part_left = lax.dynamic_slice_in_dim(left_panel, first_row, span_rows, 3)]
  transfers between devices with their start and end apart: 2 -> 2, of which waited for: 2 -> 2; matrix products, arithmetic and copies ran while one was open for 1% -> 4% of each run, Pallas kernels for 0% -> 0%
where the time goes in v1:
time: 263 us; the launch traced here: 261 us
  waiting for transfers between devices  116 us (44%)
  local copies, waits for them, and re-layouts  82.3 us (31%)
  other arithmetic  21.9 us (8%)
  matrix products  13.9 us (5%)
  between operations  13.4 us (5%)
  starting transfers between devices  11 us (4%)
  loops' own time  3.12 us (1%)
    all_to_all x1, waiting for transfers between devices, shards(): left_panel = lax.all_to_all(copies, 'rcv', 3, 3, tiled=True)  96.8 us
    dynamic_slice x64, local copies, waits for them, and re-layouts, block_terms(): part_left = lax.dynamic_slice_in_dim(left_panel, first_row, span_rows, 3)  36.4 us
    dynamic_slice x32, local copies, waits for them, and re-layouts, add_block(): portion = lax.dynamic_slice_in_dim(incoming, first_row, span_rows, 2)  31.2 us
    all_gather x1, waiting for transfers between devices, shards(): incoming = lax.all_gather(recorded, 'src', axis=2, tiled=True)  18.9 us
    dot_general x32, matrix products, block_terms(): jnp.einsum('fastik,fbktj->fabstij', scaled, right_tiles, preferred_elemen...  13.9 us
    unnamed x11, local copies, waits for them, and re-layouts  11.5 us
    all_to_all x1, starting transfers between devices, shards(): left_panel = lax.all_to_all(copies, 'rcv', 3, 3, tiled=True)  11 us
    add x32, other arithmetic, add_block(): return running + block_terms(portion, first_row, span_rows, weights)  10.7 us
  transfers between devices with their start and end apart: 2, of which 2 were waited for; matrix products, arithmetic and copies ran while one was open for 4% of the time, Pallas kernels for 0%

profile of v1, /device:TPU:1, one launch (start us, length us, event | category | flops | bytes accessed | tf_op | source)
XLA Modules:
  0.0 261.4 jit_solution(6966141159085065373)
XLA Ops:
  6.5 2.0 copy.29
  8.6 1.4 copy.30
  10.0 1.2 constant_dynamic-update-slice_fusion.7
  11.1 1.2 constant_dynamic-update-slice_fusion.6
  12.3 1.1 constant_dynamic-update-slice_fusion.5
  13.5 1.1 constant_dynamic-update-slice_fusion.4
  14.6 1.2 constant_dynamic-update-slice_fusion.3
  15.8 1.2 constant_dynamic-update-slice_fusion.2
  17.0 1.1 constant_dynamic-update-slice_fusion.1
  18.1 1.2 constant_dynamic-update-slice_fusion
  19.3 11.0 %all-to-all-start = ((bf16[1,2,256,4096]{2,1,0,3:T(2,128)(2,1)}), bf16[1,2,256,4096]{2,1,0,3:T(2,128)(2,1)}, u32[]{:S(2)}, u32[]{:S(2)}) async-start(bf16[1,2,256,4096]{2,1,0,3:T(2,128)(2,1)} %constant_dynamic-update-slice_fusion), calls=%async_computation | async-start | bytes 8388608 | tf_op jit(solution)/shard_map/all_to_all | solution.py:31
  30.3 96.8 %all-to-all-done = bf16[1,2,256,4096]{2,1,0,3:T(2,128)(2,1)} async-done(((bf16[1,2,256,4096]{2,1,0,3:T(2,128)(2,1)}), bf16[1,2,256,4096]{2,1,0,3:T(2,128)(2,1)}, u32[]{:S(2)}, u32[]{:S(2)}) %all-to-all-start) | async-done | bytes 4194336 | tf_op jit(solution)/shard_map/all_to_all | solution.py:31
  127.1 18.9 %all-gather.2.cloned.1.call-done = bf16[1,2,4096,512]{2,3,1,0:T(8,128)(2,1)} async-done(((bf16[1,2,256,512]{2,3,1,0:T(8,128)(2,1)}), bf16[1,2,4096,512]{2,3,1,0:T(8,128)(2,1)}) %all-gather.2.cloned.1.call-update) | async-done | bytes 8388624 | tf_op jit(solution)/shard_map/all_gather | solution.py:54
  146.0 106.7 %while.16 = (s32[]{:T(128)}, f32[1,2,2,4,128,128]{4,5,2,3,1,0:T(8,128)S(1)}, bf16[1,2,4096,512]{2,3,1,0:T(8,128)(2,1)}, bf16[1,2,256,4096]{2,1,0,3:T(2,128)(2,1)...) while((s32[]{:T(128)}, ...), condition=%wide.region_2.3_spmd.clone, body=%wide.region_0.2_spmd.clone.sunk | while | flops 135929600 | bytes 10382649 | solution.py:62
  149.3 1.0 constant_dynamic-slice_fusion.4
  152.6 1.0 constant_dynamic-slice_fusion.4
  156.0 1.0 constant_dynamic-slice_fusion.4
  159.3 1.0 constant_dynamic-slice_fusion.4
  162.6 1.0 constant_dynamic-slice_fusion.4
  166.0 1.0 constant_dynamic-slice_fusion.4
  169.3 1.0 constant_dynamic-slice_fusion.4
  172.6 1.0 constant_dynamic-slice_fusion.4
  189.3 1.0 constant_dynamic-slice_fusion.4
  199.3 1.0 constant_dynamic-slice_fusion.4
  209.3 1.0 constant_dynamic-slice_fusion.4
  216.0 1.0 constant_dynamic-slice_fusion.4
  219.4 1.0 constant_dynamic-slice_fusion.4
  226.0 1.0 constant_dynamic-slice_fusion.4
  236.0 1.0 constant_dynamic-slice_fusion.4
  239.4 1.0 constant_dynamic-slice_fusion.4
  246.0 1.0 constant_dynamic-slice_fusion.4
  253.1 1.4 reshape.136
  (406 shorter events, 87.0 us)
Async XLA Ops:
  6.5 139.4 %all-gather.2.cloned.1.call-start = ((), (), s32[]{:S(2)}) async-start(), calls=%async_computation.1 | async-start | bytes 8912896 | tf_op jit(solution)/shard_map/all_gather | solution.py:54
  19.3 11.0 %copy-start = (s32[2,4,3]{1,0,2:T(2,128)S(1)}, s32[2,4,3]{1,0,2:T(2,128)}, u32[]{:S(2)}) copy-start(s32[2,4,3]{1,0,2:T(2,128)} %param.5) | copy-start | bytes 292
  19.3 107.8 %all-to-all-start = ((bf16[1,2,256,4096]{2,1,0,3:T(2,128)(2,1)}), bf16[1,2,256,4096]{2,1,0,3:T(2,128)(2,1)}, u32[]{:S(2)}, u32[]{:S(2)}) async-start(bf16[1,2,256,4096]{2,1,0,3:T(2,128)(2,1)} %constant_dynamic-update-slice_fusion), calls=%async_computation | async-start | bytes 8388608 | tf_op jit(solution)/shard_map/all_to_all | solution.py:31
Sparse Core Ops, SparseCore 0:
  10.3 135.5 all-gather.1
